TPU v7x, 256 devices: a whole 4x4x8 slice. The times are simulated.
256 devices in a mesh: blk: 16 (over z, x_lo), head: 4 (over x_hi, core), batch: 4 (over y).
Axes of the slice: x: 4 (x_hi: 2, x_lo: 2; x = x_hi * 2 + x_lo), y: 4, z: 8, core: 2. Of those that a mesh axis runs over, the one named last changes fastest.
Arguments:
- query_rows: bfloat16 [16384, 3072], P(('batch', 'blk'), 'head'), parts along dimension 0, may hold values from -6 to 6
- key_rows: bfloat16 [16384, 3072], P(('batch', 'blk'), 'head'), parts along dimension 0, may hold values from -6 to 6
- value_rows: bfloat16 [16384, 3072], P(('batch', 'blk'), 'head'), parts along dimension 0, may hold values from -6 to 6
- query_tangent: bfloat16 [16384, 3072], P(('batch', 'blk'), 'head'), parts along dimension 0, may hold values from -6 to 6
- key_tangent: bfloat16 [16384, 3072], P(('batch', 'blk'), 'head'), parts along dimension 0, may hold values from -6 to 6
- value_tangent: bfloat16 [16384, 3072], P(('batch', 'blk'), 'head'), parts along dimension 0, may hold values from -6 to 6
Outputs:
- attended: bfloat16 [16384, 3072], P(('batch', 'blk', 'head')), parts along dimension 0
- attended_tangent: bfloat16 [16384, 3072], P(('batch', 'blk', 'head')), parts along dimension 0
There are 4 independent parts, one for each index of `batch`. A program takes and returns all parts, laid end to end along the dimension named above; each array names one. Nothing has to cross between parts.
All inputs are finite; a program needn't handle non-finite values.
Results may differ from a plain program's by a relative error of at most 0.011.
Values may be sent and summed in bfloat16 or wider, within the bound.
A program may use at most 128 MiB of HBM per device.

v0:
```python
from functools import partial
import jax
import jax.numpy as jnp
from jax import lax
from jax.sharding import PartitionSpec as P

HD = 128
LOWEST = -1e30


def score_pair(query_heads, tangent_heads, key_block, key_change, scaling):
    scores = (
        jnp.einsum("qhd,khd->qhk", query_heads, key_block, preferred_element_type=jnp.float32)
        * scaling
    )
    score_change = (
        jnp.einsum("qhd,khd->qhk", tangent_heads, key_block, preferred_element_type=jnp.float32)
        + jnp.einsum("qhd,khd->qhk", query_heads, key_change, preferred_element_type=jnp.float32)
    ) * scaling
    return (scores, score_change)


def block_update(running, members, query_heads, tangent_heads, scaling):
    row_max, row_total, row_shift, numerator, tangent_numerator = running
    key_block, value_block, key_change, value_change = members
    scores, score_change = score_pair(query_heads, tangent_heads, key_block, key_change, scaling)
    new_max = jnp.maximum(row_max, jnp.max(scores, axis=2))
    shrink = jnp.exp(row_max - new_max)
    weights = jnp.exp(scores - new_max[:, :, None])
    mixed_terms = weights * score_change
    row_total = row_total * shrink + jnp.sum(weights, axis=2)
    row_shift = row_shift * shrink + jnp.sum(mixed_terms, axis=2)
    weights_low = weights.astype(jnp.bfloat16)
    mixed_low = mixed_terms.astype(jnp.bfloat16)
    numerator = numerator * shrink[:, :, None] + jnp.einsum(
        "qhk,khd->qhd", weights_low, value_block, preferred_element_type=jnp.float32
    )
    tangent_numerator = (
        tangent_numerator * shrink[:, :, None]
        + jnp.einsum("qhk,khd->qhd", mixed_low, value_block, preferred_element_type=jnp.float32)
        + jnp.einsum("qhk,khd->qhd", weights_low, value_change, preferred_element_type=jnp.float32)
    )
    return (new_max, row_total, row_shift, numerator, tangent_numerator)


def fold_keys(running, pieces, start, query_heads, tangent_heads):
    key_count = pieces[0].shape[0]
    head_count = query_heads.shape[1]
    head_width = query_heads.shape[2]
    block_rows = key_count
    while block_rows > 1024 and block_rows % 2 == 0:
        block_rows = block_rows // 2
    stacked = tuple(
        (
            member.reshape(key_count // block_rows, block_rows, head_count, head_width)
            for member in pieces
        )
    )
    scaling = head_width ** (-0.5)

    def advance(carried, members):
        return (block_update(carried, members, query_heads, tangent_heads, scaling), None)

    running, unused = lax.scan(advance, running, stacked)
    return running


def prepare(query_rows, query_tangent):
    query_heads = query_rows.reshape(query_rows.shape[0], -1, HD)
    tangent_heads = query_tangent.reshape(query_tangent.shape[0], -1, HD)
    rows_here = query_heads.shape[0]
    head_count = query_heads.shape[1]
    zero_stats = jnp.zeros((rows_here, head_count), jnp.float32)
    zero_rows = jnp.zeros((rows_here, head_count, HD), jnp.float32)
    initial = (
        jnp.full((rows_here, head_count), LOWEST, jnp.float32),
        zero_stats,
        zero_stats,
        zero_rows,
        zero_rows,
    )
    folder = partial(fold_keys, query_heads=query_heads, tangent_heads=tangent_heads)
    return (folder, initial)


def finish(running):
    row_max, row_total, row_shift, numerator, tangent_numerator = running
    attended = numerator / row_total[:, :, None]
    attended_tangent = (
        tangent_numerator / row_total[:, :, None] - (row_shift / row_total)[:, :, None] * attended
    )
    rows_here = attended.shape[0]
    return (
        attended.reshape(rows_here, -1).astype(jnp.bfloat16),
        attended_tangent.reshape(rows_here, -1).astype(jnp.bfloat16),
    )


def local(query_rows, key_rows, value_rows, query_tangent, key_tangent, value_tangent):
    folder, initial = prepare(query_rows, query_tangent)
    running = folder(
        initial,
        (
            lax.all_gather(key_rows, "blk", axis=0, tiled=True),
            lax.all_gather(value_rows, "blk", axis=0, tiled=True),
            lax.all_gather(key_tangent, "blk", axis=0, tiled=True),
            lax.all_gather(value_tangent, "blk", axis=0, tiled=True),
        ),
        jnp.int32(0),
    )
    result_rows, result_tangent = finish(running)
    attended, attended_tangent = (
        lax.all_to_all(result_rows, "head", split_axis=0, concat_axis=1, tiled=True),
        lax.all_to_all(result_tangent, "head", split_axis=0, concat_axis=1, tiled=True),
    )
    return (attended, attended_tangent)


def solution(mesh):
    return jax.shard_map(
        local,
        mesh=mesh,
        in_specs=(
            P(("batch", "blk"), "head"),
            P(("batch", "blk"), "head"),
            P(("batch", "blk"), "head"),
            P(("batch", "blk"), "head"),
            P(("batch", "blk"), "head"),
            P(("batch", "blk"), "head"),
        ),
        out_specs=(P(("batch", "blk", "head"), None), P(("batch", "blk", "head"), None)),
        check_vma=False,
    )
```

profile of v0, /device:TPU:1, one launch (start us, length us, event | category | flops | bytes accessed | tf_op | source)
XLA Modules:
  0.0 715.6 jit_solution(13581352506316343537)
XLA Ops:
  7.2 0.7 all-gather.5.cloned.1.call-update
  7.9 0.7 all-gather.7.cloned.1.call-update
  8.7 0.7 all-gather.9.cloned.1.call-update
  9.4 0.5 all-gather.11.cloned.1.call-update
  10.0 1.2 copy.34
  11.2 0.2 copy.40
  11.4 1.2 copy.35
  12.6 0.2 copy.41
  12.8 141.1 %all-gather.5.cloned.1.call-done = bf16[4096,768]{1,0:T(8,128)(2,1)} async-done(((bf16[256,768]{1,0:T(8,128)(2,1)}), bf16[4096,768]{1,0:T(8,128)(2,1)}) %all-gather.5.cloned.1.call-update) | async-done | bytes 6291472 | tf_op jit(solution)/shard_map/all_gather | solution.py:104
  153.9 13.7 %reshape.44 = bf16[4,1024,6,128]{3,2,1,0:T(8,128)(2,1)} reshape(bf16[4096,768]{1,0:T(8,128)(2,1)} %all-gather.5.cloned.1.call-done) | data formatting | bytes 12582912 | tf_op jit(solution)/shard_map/reshape | solution.py:55
  167.6 7.5 %copy.39 = bf16[4,1024,6,128]{3,1,2,0:T(8,128)(2,1)} copy(bf16[4,1024,6,128]{3,2,1,0:T(8,128)(2,1)} %reshape.44) | data formatting | bytes 12582912
  175.1 121.9 %all-gather.7.cloned.1.call-done = bf16[4096,768]{1,0:T(8,128)(2,1)} async-done(((bf16[256,768]{1,0:T(8,128)(2,1)}), bf16[4096,768]{1,0:T(8,128)(2,1)}) %all-gather.7.cloned.1.call-update) | async-done | bytes 6291472 | tf_op jit(solution)/shard_map/all_gather | solution.py:106
  297.0 13.7 %reshape.45 = bf16[4,1024,6,128]{3,2,1,0:T(8,128)(2,1)} reshape(bf16[4096,768]{1,0:T(8,128)(2,1)} %all-gather.7.cloned.1.call-done) | data formatting | bytes 12582912 | tf_op jit(solution)/shard_map/reshape | solution.py:55
  310.7 7.5 %copy.42 = bf16[4,1024,6,128]{3,1,2,0:T(8,128)(2,1)} copy(bf16[4,1024,6,128]{3,2,1,0:T(8,128)(2,1)} %reshape.45) | data formatting | bytes 12582912
  318.2 121.9 %all-gather.9.cloned.1.call-done = bf16[4096,768]{1,0:T(8,128)(2,1)} async-done(((bf16[256,768]{1,0:T(8,128)(2,1)}), bf16[4096,768]{1,0:T(8,128)(2,1)}) %all-gather.9.cloned.1.call-update) | async-done | bytes 6291472 | tf_op jit(solution)/shard_map/all_gather | solution.py:105
  440.1 13.7 %reshape.46 = bf16[4,1024,6,128]{3,2,1,0:T(8,128)(2,1)} reshape(bf16[4096,768]{1,0:T(8,128)(2,1)} %all-gather.9.cloned.1.call-done) | data formatting | bytes 12582912 | tf_op jit(solution)/shard_map/reshape | solution.py:55
  453.8 11.5 %copy.43 = bf16[4,1024,6,128]{1,3,2,0:T(8,128)(2,1)} copy(bf16[4,1024,6,128]{3,2,1,0:T(8,128)(2,1)} %reshape.46) | data formatting | bytes 12582912
  465.3 117.8 %all-gather.11.cloned.1.call-done = bf16[4096,768]{1,0:T(8,128)(2,1)} async-done(((bf16[256,768]{1,0:T(8,128)(2,1)}), bf16[4096,768]{1,0:T(8,128)(2,1)}) %all-gather.11.cloned.1.call-update) | async-done | bytes 6291472 | tf_op jit(solution)/shard_map/all_gather | solution.py:107
  583.0 13.7 %reshape.47 = bf16[4,1024,6,128]{3,2,1,0:T(8,128)(2,1)} reshape(bf16[4096,768]{1,0:T(8,128)(2,1)} %all-gather.11.cloned.1.call-done) | data formatting | bytes 12582912 | tf_op jit(solution)/shard_map/reshape | solution.py:55
  596.7 11.4 %copy.44 = bf16[4,1024,6,128]{1,3,2,0:T(8,128)(2,1)} copy(bf16[4,1024,6,128]{3,2,1,0:T(8,128)(2,1)} %reshape.47) | data formatting | bytes 12582912
  608.1 72.6 %while.19 = (s32[]{:T(128)}, f32[256,6]{0,1:T(8,128)S(1)}, f32[256,6]{0,1:T(8,128)S(1)}, f32[256,6]{0,1:T(8,128)S(1)}, f32[256,6,128]{0,2,1:T(8,128)S(1)}, /*ind...) while((s32[]{:T(128)}, f32[256,6]{0,1:T(8,128)S(1)}, ...), condition=%wide.region_4.5_spmd.clone, body=%wide.region_0.4_spmd.clone.sunk | while | flops 2445617664 | bytes 109863144 | solution.py:64
  608.1 5.0 bitcast_reduce_fusion.2
  613.2 2.5 fusion.90
  615.8 0.7 copy-done
  616.5 4.0 fusion.91
  620.5 0.6 fusion.95
  621.2 2.7 fusion.96
  623.9 1.4 fusion.94
  625.2 1.0 fusion.89
  626.3 5.1 bitcast_reduce_fusion.2
  631.4 2.5 fusion.90
  633.9 0.7 copy-done
  634.6 4.0 fusion.91
  638.7 0.6 fusion.95
  639.3 2.7 fusion.96
  642.0 1.4 fusion.94
  643.4 1.0 fusion.89
  644.4 5.1 bitcast_reduce_fusion.2
  649.5 2.5 fusion.90
  652.0 0.7 copy-done
  652.7 4.0 fusion.91
  656.8 0.6 fusion.95
  657.5 2.7 fusion.96
  660.1 1.4 fusion.94
  661.5 1.0 fusion.89
  662.6 5.1 bitcast_reduce_fusion.2
  667.6 2.5 fusion.90
  670.2 0.7 copy-done
  670.9 4.0 fusion.91
  675.0 0.6 fusion.95
  675.6 2.7 fusion.96
  678.3 1.4 fusion.94
  679.7 1.0 fusion.89
  680.7 0.2 subtract_convert_fusion
  680.9 0.3 copy.45
  681.3 1.2 convert_element_type.21
  682.5 5.3 all-to-all-start
  687.8 0.3 copy.47
  688.1 1.2 convert_element_type.23
  689.4 6.5 all-to-all-done
  695.9 4.3 all-to-all-start.1
  700.2 0.8 copy.60
  701.0 7.3 %all-to-all-done.1 = bf16[4,64,768]{2,1,0:T(8,128)(2,1)S(1)} async-done(((bf16[4,64,768]{2,1,0:T(8,128)(2,1)}), bf16[4,64,768]{2,1,0:T(8,128)(2,1)S(1)}, u32[]{:S(2)}, u32[]{:S(2)}) %all-to-all-start.1) | async-done | bytes 393248 | tf_op jit(solution)/shard_map/all_to_all | solution.py:114
  708.3 0.8 copy.61
  (50 shorter events, 0.3 us)
Async XLA Ops:
  7.2 146.8 %all-gather.5.cloned.1.call-start = ((), (), s32[]{:S(2)}) async-start(), calls=%async_computation.2 | async-start | bytes 6684672 | tf_op jit(solution)/shard_map/all_gather | solution.py:104
  7.9 289.1 %all-gather.7.cloned.1.call-start = ((), (), s32[]{:S(2)}) async-start(), calls=%async_computation.3 | async-start | bytes 6684672 | tf_op jit(solution)/shard_map/all_gather | solution.py:106
  8.6 431.4 %all-gather.9.cloned.1.call-start = ((), (), s32[]{:S(2)}) async-start(), calls=%async_computation.4 | async-start | bytes 6684672 | tf_op jit(solution)/shard_map/all_gather | solution.py:105
  9.4 573.6 %all-gather.11.cloned.1.call-start = ((), (), s32[]{:S(2)}) async-start(), calls=%async_computation.5 | async-start | bytes 6684672 | tf_op jit(solution)/shard_map/all_gather | solution.py:107
  613.2 3.3 copy-start
  613.2 7.3 %slice-start = ((s8[6291456]{0:T(1024)(128)(4,1)}), s8[4194304]{0:T(1024)(128)(4,1)S(1)}, s32[]{:S(2)}) async-start(s8[6291456]{0:T(1024)(128)(4,1)} %bitcast.105), calls=%async_computation.6 | async-start | bytes 8388608 | tf_op jit(solution)/shard_map/while
  616.5 4.1 slice-start.1
  631.3 3.3 copy-start
  631.3 7.3 %slice-start = ((s8[6291456]{0:T(1024)(128)(4,1)}), s8[4194304]{0:T(1024)(128)(4,1)S(1)}, s32[]{:S(2)}) async-start(s8[6291456]{0:T(1024)(128)(4,1)} %bitcast.105), calls=%async_computation.6 | async-start | bytes 8388608 | tf_op jit(solution)/shard_map/while
  634.6 4.1 slice-start.1
  649.5 3.3 copy-start
  649.5 7.3 %slice-start = ((s8[6291456]{0:T(1024)(128)(4,1)}), s8[4194304]{0:T(1024)(128)(4,1)S(1)}, s32[]{:S(2)}) async-start(s8[6291456]{0:T(1024)(128)(4,1)} %bitcast.105), calls=%async_computation.6 | async-start | bytes 8388608 | tf_op jit(solution)/shard_map/while
  652.7 4.1 slice-start.1
  667.6 3.3 copy-start
  667.6 7.3 %slice-start = ((s8[6291456]{0:T(1024)(128)(4,1)}), s8[4194304]{0:T(1024)(128)(4,1)S(1)}, s32[]{:S(2)}) async-start(s8[6291456]{0:T(1024)(128)(4,1)} %bitcast.105), calls=%async_computation.6 | async-start | bytes 8388608 | tf_op jit(solution)/shard_map/while
  670.9 4.1 slice-start.1
  682.5 13.4 %all-to-all-start = ((bf16[4,64,768]{2,1,0:T(8,128)(2,1)}), bf16[4,64,768]{2,1,0:T(8,128)(2,1)S(1)}, u32[]{:S(2)}, u32[]{:S(2)}) async-start(bf16[4,64,768]{2,1,0:T(8,128)(2,1)} %convert_element_type.21), calls=%async_computation | async-start | bytes 786432 | tf_op jit(solution)/shard_map/all_to_all | solution.py:113
  695.9 12.4 %all-to-all-start.1 = ((bf16[4,64,768]{2,1,0:T(8,128)(2,1)}), bf16[4,64,768]{2,1,0:T(8,128)(2,1)S(1)}, u32[]{:S(2)}, u32[]{:S(2)}) async-start(bf16[4,64,768]{2,1,0:T(8,128)(2,1)} %convert_element_type.23), calls=%async_computation.1 | async-start | bytes 786432 | tf_op jit(solution)/shard_map/all_to_all | solution.py:114
Sparse Core Ops, SparseCore 0:
  9.8 144.0 all-gather.4
  155.7 141.2 all-gather.6
  298.8 141.2 all-gather.8
  441.7 141.2 all-gather.10
where the time goes:
time: 718 us; the launch traced here: 716 us
  waiting for transfers between devices  519 us (72%)
  local copies, waits for them, and re-layouts  103 us (14%)
  matrix products  65.1 us (9%)
  between operations  13.9 us (2%)
  starting transfers between devices  9.79 us (1%)
    all_gather x1, waiting for transfers between devices, local(): lax.all_gather(key_rows, 'blk', axis=0, tiled=True)  141 us
    all_gather x1, waiting for transfers between devices, local(): lax.all_gather(value_rows, 'blk', axis=0, tiled=True)  122 us
    all_gather x1, waiting for transfers between devices, local(): lax.all_gather(key_tangent, 'blk', axis=0, tiled=True)  122 us
    all_gather x1, waiting for transfers between devices, local(): lax.all_gather(value_tangent, 'blk', axis=0, tiled=True)  118 us
    reshape x4, local copies, waits for them, and re-layouts, fold_keys(): member.reshape(key_count // block_rows, block_rows, head_count, head_width)  54.7 us
    unnamed x8, local copies, waits for them, and re-layouts  40.7 us
    dot_general x4, matrix products, score_pair(): jnp.einsum('qhd,khd->qhk', query_heads, key_block, preferred_element_type...  20.2 us
    dot_general x4, matrix products, score_pair(): jnp.einsum('qhd,khd->qhk', query_heads, key_change, preferred_element_typ...  16.1 us
  transfers between devices with their start and end apart: 6, of which 6 were waited for; matrix products, arithmetic and copies ran while one was open for 10% of the time, Pallas kernels for 0%

commit v1 on v0

--- a/solution.py
+++ b/solution.py
@@ -104,7 +104,10 @@
             lax.all_gather(key_rows, "blk", axis=0, tiled=True),
             lax.all_gather(value_rows, "blk", axis=0, tiled=True),
             lax.all_gather(key_tangent, "blk", axis=0, tiled=True),
-            lax.all_gather(value_tangent, "blk", axis=0, tiled=True),
+            jnp.concatenate(
+                lax.all_to_all(jnp.stack([value_tangent] * lax.axis_size("blk")), "blk", 0, 0),
+                axis=0,
+            ),
         ),
         jnp.int32(0),
     )

time: 718 us -> 678 us (0.944)
  waiting for transfers between devices: 519 us -> 465 us
  starting transfers between devices: 9.79 us -> 20 us
    all_to_all x0 -> x1, waiting for transfers between devices: none -> 176 us  [local(): lax.all_to_all(jnp.stack([value_tangent] * lax.axis_size('blk')), 'blk',...]
    all_gather x1 -> x0, waiting for transfers between devices: 118 us -> none  [local(): lax.all_gather(value_tangent, 'blk', axis=0, tiled=True)]
    all_gather x1, waiting for transfers between devices: 141 us -> 30.9 us  [local(): lax.all_gather(key_rows, 'blk', axis=0, tiled=True)]
    another operation x0 -> x2, local copies, waits for them, and re-layouts: none -> 13.5 us  [the longest x1 10.2 us: fold_keys(): member.reshape(key_count // block_rows, block_rows, head_count, head_width)]
    reshape x4 -> x3, local copies, waits for them, and re-layouts: 54.7 us -> 41.3 us  [fold_keys(): member.reshape(key_count // block_rows, block_rows, head_count, head_width)]
    all_to_all x0 -> x1, starting transfers between devices: none -> 10.2 us  [local(): lax.all_to_all(jnp.stack([value_tangent] * lax.axis_size('blk')), 'blk',...]
    all_to_all x0 -> x1, local copies, waits for them, and re-layouts: none -> 9.07 us  [local(): lax.all_to_all(jnp.stack([value_tangent] * lax.axis_size('blk')), 'blk',...]
    unnamed x8 -> x13, local copies, waits for them, and re-layouts: 40.7 us -> 35.7 us
  transfers between devices with their start and end apart: 6 -> 6, of which waited for: 6 -> 6; matrix products, arithmetic and copies ran while one was open for 10% -> 11% of each run, Pallas kernels for 0% -> 0%
where the time goes in v1:
time: 678 us; the launch traced here: 676 us
  waiting for transfers between devices  465 us (69%)
  local copies, waits for them, and re-layouts  107 us (16%)
  matrix products  65.2 us (10%)
  starting transfers between devices  20 us (3%)
  between operations  13.9 us (2%)
    all_to_all x1, waiting for transfers between devices, local(): lax.all_to_all(jnp.stack([value_tangent] * lax.axis_size('blk')), 'blk',...  176 us
    all_gather x1, waiting for transfers between devices, local(): lax.all_gather(value_rows, 'blk', axis=0, tiled=True)  122 us
    all_gather x1, waiting for transfers between devices, local(): lax.all_gather(key_tangent, 'blk', axis=0, tiled=True)  120 us
    reshape x3, local copies, waits for them, and re-layouts, fold_keys(): member.reshape(key_count // block_rows, block_rows, head_count, head_width)  41.3 us
    unnamed x13, local copies, waits for them, and re-layouts  35.7 us
    all_gather x1, waiting for transfers between devices, local(): lax.all_gather(key_rows, 'blk', axis=0, tiled=True)  30.9 us
    dot_general x4, matrix products, score_pair(): jnp.einsum('qhd,khd->qhk', query_heads, key_block, preferred_element_type...  20.4 us
    dot_general x4, matrix products, score_pair(): jnp.einsum('qhd,khd->qhk', query_heads, key_change, preferred_element_typ...  16.1 us
  transfers between devices with their start and end apart: 6, of which 6 were waited for; matrix products, arithmetic and copies ran while one was open for 11% of the time, Pallas kernels for 0%

profile of v1, /device:TPU:1, one launch (start us, length us, event | category | flops | bytes accessed | tf_op | source)
XLA Modules:
  0.0 675.8 jit_solution(4746782658757693137)
XLA Ops:
  7.2 0.7 all-gather.4.cloned.1.call-update
  7.9 0.7 all-gather.6.cloned.1.call-update
  8.6 1.2 copy.57
  9.8 3.3 stack.2
  13.1 10.2 %all-to-all-start = ((bf16[16,256,768]{1,2,0:T(8,128)(2,1)}), bf16[16,256,768]{1,2,0:T(8,128)(2,1)}, u32[]{:S(2)}, u32[]{:S(2)}) async-start(bf16[16,256,768]{1,2,0:T(8,128)(2,1)} %stack.2), calls=%async_computation | async-start | bytes 12582912 | tf_op jit(solution)/shard_map/all_to_all | solution.py:108
  23.4 0.7 all-gather.8.cloned.1.call-update
  24.3 0.2 copy.60
  24.8 0.2 copy.61
  25.0 176.0 %all-to-all-done = bf16[16,256,768]{1,2,0:T(8,128)(2,1)} async-done(((bf16[16,256,768]{1,2,0:T(8,128)(2,1)}), bf16[16,256,768]{1,2,0:T(8,128)(2,1)}, u32[]{:S(2)}, u32[]{:S(2)}) %all-to-all-start) | async-done | bytes 6291488 | tf_op jit(solution)/shard_map/all_to_all | solution.py:108
  201.0 9.1 %copy.58 = bf16[16,256,768]{1,0,2:T(8,128)(2,1)} copy(bf16[16,256,768]{1,2,0:T(8,128)(2,1)} %all-to-all-done) | data formatting | bytes 12582912 | tf_op jit(solution)/shard_map/all_to_all | solution.py:108
  210.1 10.2 %reshape_reshape.3 = bf16[4,1024,6,128]{1,0,3,2:T(4,128)(2,1)} reshape(bf16[16,256,768]{1,0,2:T(8,128)(2,1)} %copy.58) | data formatting | bytes 12582912 | tf_op jit(solution)/shard_map/reshape;reshape | solution.py:55
  220.2 7.5 %copy.64 = bf16[4,1024,6,128]{1,3,2,0:T(8,128)(2,1)} copy(bf16[4,1024,6,128]{1,0,3,2:T(4,128)(2,1)} %reshape_reshape.3) | data formatting | bytes 12582912
  227.7 30.9 %all-gather.4.cloned.1.call-done = bf16[4096,768]{1,0:T(8,128)(2,1)} async-done(((bf16[256,768]{1,0:T(8,128)(2,1)}), bf16[4096,768]{1,0:T(8,128)(2,1)}) %all-gather.4.cloned.1.call-update) | async-done | bytes 6291472 | tf_op jit(solution)/shard_map/all_gather | solution.py:104
  258.6 13.8 %reshape.42 = bf16[4,1024,6,128]{3,2,1,0:T(8,128)(2,1)} reshape(bf16[4096,768]{1,0:T(8,128)(2,1)} %all-gather.4.cloned.1.call-done) | data formatting | bytes 12582912 | tf_op jit(solution)/shard_map/reshape | solution.py:55
  272.4 7.4 %copy.59 = bf16[4,1024,6,128]{3,1,2,0:T(8,128)(2,1)} copy(bf16[4,1024,6,128]{3,2,1,0:T(8,128)(2,1)} %reshape.42) | data formatting | bytes 12582912
  279.8 120.2 %all-gather.6.cloned.1.call-done = bf16[4096,768]{1,0:T(8,128)(2,1)} async-done(((bf16[256,768]{1,0:T(8,128)(2,1)}), bf16[4096,768]{1,0:T(8,128)(2,1)}) %all-gather.6.cloned.1.call-update) | async-done | bytes 6291472 | tf_op jit(solution)/shard_map/all_gather | solution.py:106
  400.0 13.8 %reshape.43 = bf16[4,1024,6,128]{3,2,1,0:T(8,128)(2,1)} reshape(bf16[4096,768]{1,0:T(8,128)(2,1)} %all-gather.6.cloned.1.call-done) | data formatting | bytes 12582912 | tf_op jit(solution)/shard_map/reshape | solution.py:55
  413.7 7.4 %copy.62 = bf16[4,1024,6,128]{3,1,2,0:T(8,128)(2,1)} copy(bf16[4,1024,6,128]{3,2,1,0:T(8,128)(2,1)} %reshape.43) | data formatting | bytes 12582912
  421.1 121.9 %all-gather.8.cloned.1.call-done = bf16[4096,768]{1,0:T(8,128)(2,1)} async-done(((bf16[256,768]{1,0:T(8,128)(2,1)}), bf16[4096,768]{1,0:T(8,128)(2,1)}) %all-gather.8.cloned.1.call-update) | async-done | bytes 6291472 | tf_op jit(solution)/shard_map/all_gather | solution.py:105
  543.0 13.8 %reshape.44 = bf16[4,1024,6,128]{3,2,1,0:T(8,128)(2,1)} reshape(bf16[4096,768]{1,0:T(8,128)(2,1)} %all-gather.8.cloned.1.call-done) | data formatting | bytes 12582912 | tf_op jit(solution)/shard_map/reshape | solution.py:55
  556.8 11.5 %copy.63 = bf16[4,1024,6,128]{1,3,2,0:T(8,128)(2,1)} copy(bf16[4,1024,6,128]{3,2,1,0:T(8,128)(2,1)} %reshape.44) | data formatting | bytes 12582912
  568.2 72.7 %while.19 = (s32[]{:T(128)}, f32[256,6]{0,1:T(8,128)S(1)}, f32[256,6]{0,1:T(8,128)S(1)}, f32[256,6]{0,1:T(8,128)S(1)}, f32[256,6,128]{0,2,1:T(8,128)S(1)}, /*ind...) while((s32[]{:T(128)}, f32[256,6]{0,1:T(8,128)S(1)}, ...), condition=%wide.region_4.5_spmd.clone, body=%wide.region_0.4_spmd.clone.sunk | while | flops 2445617664 | bytes 109863144 | solution.py:64
  568.2 5.1 bitcast_reduce_fusion.2
  573.4 2.5 fusion.90
  575.9 0.7 copy-done
  576.6 4.0 fusion.91
  580.7 0.6 fusion.95
  581.3 2.7 fusion.96
  584.0 1.4 fusion.94
  585.4 1.0 fusion.89
  586.4 5.1 bitcast_reduce_fusion.2
  591.5 2.5 fusion.90
  594.1 0.7 copy-done
  594.8 4.0 fusion.91
  598.9 0.6 fusion.95
  599.5 2.7 fusion.96
  602.2 1.4 fusion.94
  603.5 1.0 fusion.89
  604.6 5.1 bitcast_reduce_fusion.2
  609.7 2.5 fusion.90
  612.3 0.7 copy-done
  613.0 4.0 fusion.91
  617.1 0.6 fusion.95
  617.7 2.7 fusion.96
  620.4 1.4 fusion.94
  621.7 1.0 fusion.89
  622.8 5.1 bitcast_reduce_fusion.2
  627.9 2.5 fusion.90
  630.5 0.7 copy-done
  631.2 4.0 fusion.91
  635.3 0.6 fusion.95
  635.9 2.7 fusion.96
  638.6 1.4 fusion.94
  639.9 1.0 fusion.89
  641.2 0.3 copy.65
  641.5 1.2 convert_element_type.21
  642.7 5.3 all-to-all-start.1
  648.1 0.3 copy.67
  648.4 1.2 convert_element_type.23
  649.6 6.5 all-to-all-done.1
  656.2 4.3 all-to-all-start.2
  660.5 0.8 copy.78
  661.2 7.3 %all-to-all-done.2 = bf16[4,64,768]{2,1,0:T(8,128)(2,1)S(1)} async-done(((bf16[4,64,768]{2,1,0:T(8,128)(2,1)}), bf16[4,64,768]{2,1,0:T(8,128)(2,1)S(1)}, u32[]{:S(2)}, u32[]{:S(2)}) %all-to-all-start.2) | async-done | bytes 393248 | tf_op jit(solution)/shard_map/all_to_all | solution.py:117
  668.5 0.8 copy.79
  (56 shorter events, 0.8 us)
Async XLA Ops:
  7.2 251.5 %all-gather.4.cloned.1.call-start = ((), (), s32[]{:S(2)}) async-start(), calls=%async_computation.3 | async-start | bytes 6684672 | tf_op jit(solution)/shard_map/all_gather | solution.py:104
  7.9 392.1 %all-gather.6.cloned.1.call-start = ((), (), s32[]{:S(2)}) async-start(), calls=%async_computation.4 | async-start | bytes 6684672 | tf_op jit(solution)/shard_map/all_gather | solution.py:106
  13.1 11.0 %copy-start.1 = (bf16[256,768]{1,0:T(8,128)(2,1)S(1)}, bf16[256,768]{1,0:T(8,128)(2,1)}, u32[]{:S(2)}) copy-start(bf16[256,768]{1,0:T(8,128)(2,1)} %param.8) | copy-start | bytes 1179652
  13.1 11.4 %copy-start.2 = (bf16[256,768]{1,0:T(8,128)(2,1)S(1)}, bf16[256,768]{1,0:T(8,128)(2,1)}, u32[]{:S(2)}) copy-start(bf16[256,768]{1,0:T(8,128)(2,1)} %param.11) | copy-start | bytes 1179652
  13.1 187.8 %all-to-all-start = ((bf16[16,256,768]{1,2,0:T(8,128)(2,1)}), bf16[16,256,768]{1,2,0:T(8,128)(2,1)}, u32[]{:S(2)}, u32[]{:S(2)}) async-start(bf16[16,256,768]{1,2,0:T(8,128)(2,1)} %stack.2), calls=%async_computation | async-start | bytes 12582912 | tf_op jit(solution)/shard_map/all_to_all | solution.py:108
  23.4 519.7 %all-gather.8.cloned.1.call-start = ((), (), s32[]{:S(2)}) async-start(), calls=%async_computation.5 | async-start | bytes 6684672 | tf_op jit(solution)/shard_map/all_gather | solution.py:105
  573.3 3.3 copy-start
  573.4 7.3 %slice-start = ((s8[6291456]{0:T(1024)(128)(4,1)}), s8[4194304]{0:T(1024)(128)(4,1)S(1)}, s32[]{:S(2)}) async-start(s8[6291456]{0:T(1024)(128)(4,1)} %bitcast.107), calls=%async_computation.6 | async-start | bytes 8388608 | tf_op jit(solution)/shard_map/while
  576.6 4.1 slice-start.1
  591.5 3.3 copy-start
  591.5 7.3 %slice-start = ((s8[6291456]{0:T(1024)(128)(4,1)}), s8[4194304]{0:T(1024)(128)(4,1)S(1)}, s32[]{:S(2)}) async-start(s8[6291456]{0:T(1024)(128)(4,1)} %bitcast.107), calls=%async_computation.6 | async-start | bytes 8388608 | tf_op jit(solution)/shard_map/while
  594.8 4.1 slice-start.1
  609.7 3.3 copy-start
  609.7 7.3 %slice-start = ((s8[6291456]{0:T(1024)(128)(4,1)}), s8[4194304]{0:T(1024)(128)(4,1)S(1)}, s32[]{:S(2)}) async-start(s8[6291456]{0:T(1024)(128)(4,1)} %bitcast.107), calls=%async_computation.6 | async-start | bytes 8388608 | tf_op jit(solution)/shard_map/while
  613.0 4.1 slice-start.1
  627.9 3.3 copy-start
  627.9 7.3 %slice-start = ((s8[6291456]{0:T(1024)(128)(4,1)}), s8[4194304]{0:T(1024)(128)(4,1)S(1)}, s32[]{:S(2)}) async-start(s8[6291456]{0:T(1024)(128)(4,1)} %bitcast.107), calls=%async_computation.6 | async-start | bytes 8388608 | tf_op jit(solution)/shard_map/while
  631.2 4.1 slice-start.1
  642.7 13.4 %all-to-all-start.1 = ((bf16[4,64,768]{2,1,0:T(8,128)(2,1)}), bf16[4,64,768]{2,1,0:T(8,128)(2,1)S(1)}, u32[]{:S(2)}, u32[]{:S(2)}) async-start(bf16[4,64,768]{2,1,0:T(8,128)(2,1)} %convert_element_type.21), calls=%async_computation.1 | async-start | bytes 786432 | tf_op jit(solution)/shard_map/all_to_all | solution.py:116
  656.2 12.4 %all-to-all-start.2 = ((bf16[4,64,768]{2,1,0:T(8,128)(2,1)}), bf16[4,64,768]{2,1,0:T(8,128)(2,1)S(1)}, u32[]{:S(2)}, u32[]{:S(2)}) async-start(bf16[4,64,768]{2,1,0:T(8,128)(2,1)} %convert_element_type.23), calls=%async_computation.2 | async-start | bytes 786432 | tf_op jit(solution)/shard_map/all_to_all | solution.py:117
Sparse Core Ops, SparseCore 0:
  9.8 248.8 all-gather.3
  260.4 139.4 all-gather.5
  401.7 141.2 all-gather.7
